TPU v7x, 1024 devices: a whole 8x8x8 slice. The times are simulated.
1024 devices in a mesh: energy: 64 (over z_hi, y, core), mom: 16 (over z_lo, x).
Axes of the slice: x: 8, y: 8, z: 8 (z_hi: 4, z_lo: 2; z = z_hi * 2 + z_lo), core: 2. Of those that a mesh axis runs over, the one named last changes fastest.
Arguments:
- green: bfloat16 [16, 64, 4, 2, 256, 256], P('mom', 'energy'), may hold values from -6 to 6
- coupling: bfloat16 [2, 256, 256], replicated, may hold values from -0.375 to 0.375
- phonon: bfloat16 [3, 1024, 256], replicated, may hold values from -4 to 4
- shift: int32 [3, 2], replicated, may hold values from 0 to 1
Outputs:
- sigma: bfloat16 [16, 64, 4, 2, 256, 256], P('mom', 'energy')
All inputs are finite; a program needn't handle non-finite values.
Results may differ from a plain program's by a relative error of at most 0.0049.
Values may be sent and summed in bfloat16 or wider, within the bound.
A program may use at most 64 MiB of HBM per device.

v0:
```python
import jax
import jax.numpy as jnp
from jax import lax
from jax.sharding import PartitionSpec as P

NO = 256
MODES = 2
SMAX = 1
E_OUT = 4


def passed_along(x, axis, by):
    length = lax.axis_size(axis)
    pairs = [(i, i + by) for i in range(length) if 0 <= i + by < length]
    return lax.ppermute(x, axis, pairs)


def passed_along_2(x, axis, by):
    length = lax.axis_size(axis)
    return lax.ppermute(x, axis, [(i, (i + by) % length) for i in range(length)])


def contribution(block, weights, shift_row, coupling):
    weights = weights.reshape(MODES, 2, NO, NO)
    real_total = jnp.zeros((E_OUT, NO, NO), jnp.float32)
    imag_total = jnp.zeros((E_OUT, NO, NO), jnp.float32)
    for mode_index in range(MODES):
        first_slot = SMAX - shift_row[mode_index]
        window = lax.dynamic_slice_in_dim(block, first_slot, E_OUT, 0)
        left_product = jnp.einsum(
            "xy,ecyz->ecxz", coupling[mode_index], window, preferred_element_type=jnp.float32
        ).astype(jnp.bfloat16)
        product = jnp.dot(
            left_product.reshape(E_OUT * 2 * NO, NO),
            coupling[mode_index],
            preferred_element_type=jnp.float32,
        ).reshape(E_OUT, 2, NO, NO)
        real_total = real_total + (
            product[:, 0] * weights[mode_index, 0] - product[:, 1] * weights[mode_index, 1]
        )
        imag_total = imag_total + (
            product[:, 0] * weights[mode_index, 1] + product[:, 1] * weights[mode_index, 0]
        )
    return (real_total, imag_total)


def body(green, coupling, phonon, shift):
    own_slots = green[0, 0]
    below = passed_along(own_slots[E_OUT - SMAX :], "energy", 1)
    own_block = jnp.concatenate([below, own_slots], axis=0)
    offsets = phonon.shape[0]
    radius = (offsets - 1) // 2
    real_sum = jnp.zeros((E_OUT, NO, NO), jnp.float32)
    imag_sum = jnp.zeros((E_OUT, NO, NO), jnp.float32)
    for offset in range(offsets):
        transfer = offset - radius
        source_block = own_block if transfer == 0 else passed_along_2(own_block, "mom", transfer)
        real_term, imag_term = contribution(source_block, phonon[offset], shift[offset], coupling)
        real_sum = real_sum + real_term
        imag_sum = imag_sum + imag_term
    return jnp.stack([real_sum, imag_sum], axis=1).astype(jnp.bfloat16)[None, None]


def solution(mesh):
    placed = (P("mom", "energy", None, None, None, None), P(), P(), P())
    return jax.shard_map(
        body,
        mesh=mesh,
        in_specs=placed,
        out_specs=P("mom", "energy", None, None, None, None),
        check_vma=False,
    )
```

profile of v0, /device:TPU:287, one launch (start us, length us, event | category | flops | bytes accessed | tf_op | source)
XLA Modules:
  0.0 75.5 jit_solution(246706378840296747)
XLA Ops:
  0.0 1.0 %slice_bitcast_fusion.1 = bf16[1,2,256,256]{3,2,1,0:T(8,128)(2,1)S(1)} fusion(bf16[1,1,4,2,256,256]{5,4,3,2,1,0:T(8,128)(2,1)} %param.4), kind=kLoop, calls=%fused_computation.50 | loop fusion | bytes 524288 | tf_op jit(solution)/shard_map/slice | solution.py:49
  1.0 3.9 %collective-permute-start = (bf16[1,2,256,256]{3,2,1,0:T(8,128)(2,1)S(1)}, bf16[1,2,256,256]{3,2,1,0:T(8,128)(2,1)S(1)}, u32[]{:S(2)}, u32[]{:S(2)}) collective-permute-start(bf16[1,2,256,256]{3,2,1,0:T(8,128)(2,1)S(1)} %slice_bitcast_fusion.1), channel_id=1, source_target_pairs={{0,16},{16,32},{32,48},{48,64},{64,80},{80,96},{96,112},{112,128},... | collective-permute-start | bytes 786440 | tf_op jit(solution)/shard_map/ppermute | solution.py:15
  4.9 1.6 %fusion.81 = (s32[1,1]{0,1:T(1,128)}, s32[1,1]{0,1:T(1,128)}, s32[1,1]{0,1:T(1,128)}, s32[1,1]{0,1:T(1,128)}, s32[1,1]{0,1:T(1,128)}, /*index=5*/s32[1,1]{0,1:T(1,128)}) fusion(s32[3,2]{0,1:T(2,128)} %param.7), kind=kLoop, calls=%fused_computation.106 | loop fusion | bytes 48 | tf_op jit(solution)/shard_map/slice | solution.py:28
  14.2 1.5 %fusion.80 = (bf16[1,1024,256]{2,1,0:T(8,128)(2,1)S(1)}, bf16[1,1024,256]{2,1,0:T(8,128)(2,1)S(1)}, bf16[1,1024,256]{2,1,0:T(8,128)(2,1)S(1)}) fusion(bf16[3,1024,256]{2,1,0:T(8,128)(2,1)} %param.6), kind=kLoop, calls=%fused_computation.105 | loop fusion | bytes 3145728 | tf_op jit(solution)/shard_map/slice | solution.py:58
  15.7 1.1 %fusion.37 = (f32[256,256]{1,0:T(8,128)S(1)}, f32[256,256]{1,0:T(8,128)S(1)}, f32[256,256]{1,0:T(8,128)S(1)}, f32[256,256]{1,0:T(8,128)S(1)}, f32[256,256]{1,0:T...) fusion(bf16[2,2,256,256]{3,2,1,0:T(8,128)(2,1)S(1)} %bitcast.184, ...), kind=kLoop, calls=%fused_computation.56 | loop fusion | flops 524288 | bytes 3145728 | tf_op jit(solution)/shard_map/convert_element_type | solution.py:39
  16.8 1.4 %pad_maximum_fusion = bf16[5,2,256,256]{3,2,1,0:T(8,128)(2,1)S(1)} fusion(bf16[1,2,256,256]{3,2,1,0:T(8,128)(2,1)S(1)} %collective-permute-done, bf16[4,2,256,256]{3,2,1,0:T(8,128)(2,1)} %bitcast.186), kind=kLoop, calls=%fused_computation.2 | loop fusion | flops 655360 | bytes 2621440 | tf_op jit(solution)/shard_map/concatenate | solution.py:50
  18.3 4.7 %collective-permute-start.2 = (bf16[5,2,256,256]{3,2,1,0:T(8,128)(2,1)S(1)}, bf16[5,2,256,256]{3,2,1,0:T(8,128)(2,1)S(1)}, u32[]{:S(2)}, u32[]{:S(2)}) collective-permute-start(bf16[5,2,256,256]{3,2,1,0:T(8,128)(2,1)S(1)} %pad_maximum_fusion), channel_id=1, source_target_pairs={{0,1},{1,2},{2,3},{3,4},{4,5},{5,6},{6,7},{7,8},{8,9},{9,10},{10,1... | collective-permute-start | bytes 3932168 | tf_op jit(solution)/shard_map/ppermute | solution.py:20
  23.0 1.1 %fusion.45 = (f32[256,256]{1,0:T(8,128)}, f32[256,256]{1,0:T(8,128)}, f32[256,256]{1,0:T(8,128)}, f32[256,256]{1,0:T(8,128)}) fusion(bf16[2,2,256,256]{3,2,1,0:T(8,128)(2,1)S(1)} %bitcast.183), kind=kLoop, calls=%fused_computation.72 | loop fusion | flops 262144 | bytes 1572864 | tf_op jit(solution)/shard_map/convert_element_type | solution.py:39
  24.0 1.9 %collective-permute-start.1 = (bf16[5,2,256,256]{3,2,1,0:T(8,128)(2,1)S(1)}, bf16[5,2,256,256]{3,2,1,0:T(8,128)(2,1)S(1)}, u32[]{:S(2)}, u32[]{:S(2)}) collective-permute-start(bf16[5,2,256,256]{3,2,1,0:T(8,128)(2,1)S(1)} %pad_maximum_fusion), channel_id=1, source_target_pairs={{0,15},{1,0},{2,1},{3,2},{4,3},{5,4},{6,5},{7,6},{8,7},{9,8},{10,9... | collective-permute-start | bytes 3932168 | tf_op jit(solution)/shard_map/ppermute | solution.py:20
  26.0 0.5 fusion.4
  26.5 0.5 fusion.3
  27.0 0.4 fusion.22
  27.5 1.8 %fusion.24 = f32[4,2,256,256]{3,2,0,1:T(8,128)} fusion(bf16[4,2,256,256]{3,2,1,0:T(8,128)(2,1)S(1)} %fusion.3, bf16[2,256,256]{2,1,0:T(8,128)(2,1)S(1)} %copy-done.5), kind=kOutput, calls=%fused_computation.40 | convolution fusion | flops 268435456 | bytes 3276800 | tf_op jit(solution)/shard_map/dot_general | solution.py:33
  29.2 21.5 %collective-permute-done.2 = bf16[5,2,256,256]{3,2,1,0:T(8,128)(2,1)S(1)} collective-permute-done((bf16[5,2,256,256]{3,2,1,0:T(8,128)(2,1)S(1)}, bf16[5,2,256,256]{3,2,1,0:T(8,128)(2,1)S(1)}, u32[]{:S(2)}, u32[]{:S(2)}) %collective-permute-start.2) | collective-permute-done | bytes 1310752 | tf_op jit(solution)/shard_map/ppermute | solution.py:20
  50.7 0.4 fusion.6
  51.2 0.4 fusion.5
  51.6 1.8 %fusion.18 = f32[4,2,256,256]{3,2,0,1:T(8,128)} fusion(bf16[4,2,256,256]{3,2,1,0:T(8,128)(2,1)S(1)} %fusion.6, bf16[2,256,256]{2,1,0:T(8,128)(2,1)S(1)} %copy-done.5), kind=kOutput, calls=%fused_computation.34 | convolution fusion | flops 268435456 | bytes 3276800 | tf_op jit(solution)/shard_map/dot_general | solution.py:33
  53.4 1.7 %fusion.20 = f32[4,2,256,256]{3,2,0,1:T(8,128)} fusion(bf16[4,2,256,256]{3,2,1,0:T(8,128)(2,1)S(1)} %fusion.5, bf16[2,256,256]{2,1,0:T(8,128)(2,1)S(1)} %copy-done.5), kind=kOutput, calls=%fused_computation.36 | convolution fusion | flops 268435456 | bytes 3276800 | tf_op jit(solution)/shard_map/dot_general | solution.py:33
  55.1 2.9 %collective-permute-done.1 = bf16[5,2,256,256]{3,2,1,0:T(8,128)(2,1)S(1)} collective-permute-done((bf16[5,2,256,256]{3,2,1,0:T(8,128)(2,1)S(1)}, bf16[5,2,256,256]{3,2,1,0:T(8,128)(2,1)S(1)}, u32[]{:S(2)}, u32[]{:S(2)}) %collective-permute-start.1) | collective-permute-done | bytes 1310752 | tf_op jit(solution)/shard_map/ppermute | solution.py:20
  58.0 1.1 %copy-done.6 = bf16[5,2,256,256]{3,2,1,0:T(8,128)(2,1)} copy-done((bf16[5,2,256,256]{3,2,1,0:T(8,128)(2,1)}, bf16[5,2,256,256]{3,2,1,0:T(8,128)(2,1)S(1)}, u32[]{:S(2)}) %copy-start.6) | copy-done | bytes 1310744
  59.0 0.4 fusion.2
  59.5 1.8 %fusion.26 = f32[4,2,256,256]{3,2,0,1:T(8,128)} fusion(bf16[4,2,256,256]{3,2,1,0:T(8,128)(2,1)S(1)} %fusion.2, bf16[2,256,256]{2,1,0:T(8,128)(2,1)S(1)} %copy-done.5), kind=kOutput, calls=%fused_computation.42 | convolution fusion | flops 268435456 | bytes 3276800 | tf_op jit(solution)/shard_map/dot_general | solution.py:33
  61.3 3.3 %fusion.1 = f32[4,2,256,256]{3,2,1,0:T(8,128)} fusion(bf16[5,2,256,256]{3,2,1,0:T(8,128)(2,1)} %copy-done.6, s32[]{:T(128)S(6)} %select_n.18, bf16[2,256,256]{2,1,0:T(8,128)(2,1)S(1)} %copy-done.5), kind=kOutput, calls=%fused_computation.10 | convolution fusion | flops 537395200 | bytes 3407876 | tf_op jit(solution)/shard_map/dot_general | solution.py:33
  64.7 5.5 %fusion.33 = bf16[1,1,4,1,256,256]{5,4,2,3,1,0:T(8,128)(2,1)S(1)} fusion(f32[256,256]{1,0:T(8,128)S(1)} %get-tuple-element.17, f32[4,2,256,256]{3,2,0,1:T(8,128)} %fusion.18, f32[256,256]{1,0:T(8,128)S(1)} %get-tuple-element.18, f32[256,256]{1,0:T(8,128)S(1)} %get-tuple-element.16, f32[4,2,256,256]{3,2,0,1:T(8,128)} %fusion.20, ...), kind=kLoop, calls=%fused_computation.48 | loop fusion | flops 6291456 | bytes 16252928 | tf_op jit(solution)/shard_map/stack | solution.py:61
  70.2 0.3 copy-done.1
  70.5 0.6 copy-done.2
  71.1 0.6 copy-done.3
  71.8 0.6 copy-done.4
  72.7 0.1 copy-done.14
  72.8 1.5 %fusion.34 = bf16[1,1,4,1,256,256]{5,4,2,3,1,0:T(8,128)(2,1)S(1)} fusion(f32[256,256]{1,0:T(8,128)S(1)} %get-tuple-element.18, f32[4,2,256,256]{3,2,0,1:T(8,128)S(1)} %copy-done.1, f32[256,256]{1,0:T(8,128)S(1)} %get-tuple-element.17, f32[256,256]{1,0:T(8,128)S(1)} %get-tuple-element.19, f32[4,2,256,256]{3,2,0,1:T(8,128)S(1)} %copy-done.2, ...), kind=kLoop, calls=%fused_computation.49 | loop fusion | flops 6291456 | bytes 16252928 | tf_op jit(solution)/shard_map/stack | solution.py:61
  74.3 0.1 pad_maximum_fusion.1
  74.4 1.0 %copy.22 = bf16[1,1,4,2,256,256]{5,4,3,2,1,0:T(8,128)(2,1)} copy(bf16[1,1,4,2,256,256]{5,4,2,3,1,0:T(8,128)(2,1)S(1)} %pad_maximum_fusion.1) | data formatting | bytes 2097152 | tf_op jit(solution)/shard_map/stack | solution.py:61
  (27 shorter events, 0.4 us)
Async XLA Ops:
  1.0 15.8 %collective-permute-start = (bf16[1,2,256,256]{3,2,1,0:T(8,128)(2,1)S(1)}, bf16[1,2,256,256]{3,2,1,0:T(8,128)(2,1)S(1)}, u32[]{:S(2)}, u32[]{:S(2)}) collective-permute-start(bf16[1,2,256,256]{3,2,1,0:T(8,128)(2,1)S(1)} %slice_bitcast_fusion.1), channel_id=1, source_target_pairs={{0,16},{16,32},{32,48},{48,64},{64,80},{80,96},{96,112},{112,128},... | collective-permute-start | bytes 786440 | tf_op jit(solution)/shard_map/ppermute | solution.py:15
  16.8 9.1 %copy-start.5 = (bf16[2,256,256]{2,1,0:T(8,128)(2,1)S(1)}, bf16[2,256,256]{2,1,0:T(8,128)(2,1)}, u32[]{:S(2)}) copy-start(bf16[2,256,256]{2,1,0:T(8,128)(2,1)} %param.5) | copy-start | bytes 786436
  16.8 9.2 %copy-start.15 = (bf16[1,1,4,2,256,256]{5,4,3,2,1,0:T(8,128)(2,1)S(1)}, bf16[1,1,4,2,256,256]{5,4,3,2,1,0:T(8,128)(2,1)}, u32[]{:S(2)}) copy-start(bf16[1,1,4,2,256,256]{5,4,3,2,1,0:T(8,128)(2,1)} %param.4) | copy-start | bytes 3145732
  18.3 32.5 %collective-permute-start.2 = (bf16[5,2,256,256]{3,2,1,0:T(8,128)(2,1)S(1)}, bf16[5,2,256,256]{3,2,1,0:T(8,128)(2,1)S(1)}, u32[]{:S(2)}, u32[]{:S(2)}) collective-permute-start(bf16[5,2,256,256]{3,2,1,0:T(8,128)(2,1)S(1)} %pad_maximum_fusion), channel_id=1, source_target_pairs={{0,1},{1,2},{2,3},{3,4},{4,5},{5,6},{6,7},{7,8},{8,9},{9,10},{10,1... | collective-permute-start | bytes 3932168 | tf_op jit(solution)/shard_map/ppermute | solution.py:20
  24.0 34.0 %collective-permute-start.1 = (bf16[5,2,256,256]{3,2,1,0:T(8,128)(2,1)S(1)}, bf16[5,2,256,256]{3,2,1,0:T(8,128)(2,1)S(1)}, u32[]{:S(2)}, u32[]{:S(2)}) collective-permute-start(bf16[5,2,256,256]{3,2,1,0:T(8,128)(2,1)S(1)} %pad_maximum_fusion), channel_id=1, source_target_pairs={{0,15},{1,0},{2,1},{3,2},{4,3},{5,4},{6,5},{7,6},{8,7},{9,8},{10,9... | collective-permute-start | bytes 3932168 | tf_op jit(solution)/shard_map/ppermute | solution.py:20
  58.0 1.1 %copy-start.6 = (bf16[5,2,256,256]{3,2,1,0:T(8,128)(2,1)}, bf16[5,2,256,256]{3,2,1,0:T(8,128)(2,1)S(1)}, u32[]{:S(2)}) copy-start(bf16[5,2,256,256]{3,2,1,0:T(8,128)(2,1)S(1)} %collective-permute-done.1) | copy-start | bytes 3932164
  64.6 5.6 %copy-start = (f32[4,2,256,256]{3,2,0,1:T(8,128)S(1)}, f32[4,2,256,256]{3,2,0,1:T(8,128)}, u32[]{:S(2)}) copy-start(f32[4,2,256,256]{3,2,0,1:T(8,128)} %fusion.24) | copy-start | bytes 6291460
  64.6 5.9 %copy-start.1 = (f32[4,2,256,256]{3,2,0,1:T(8,128)S(1)}, f32[4,2,256,256]{3,2,0,1:T(8,128)}, u32[]{:S(2)}) copy-start(f32[4,2,256,256]{3,2,0,1:T(8,128)} %fusion.18) | copy-start | bytes 6291460
  64.6 6.5 %copy-start.2 = (f32[4,2,256,256]{3,2,0,1:T(8,128)S(1)}, f32[4,2,256,256]{3,2,0,1:T(8,128)}, u32[]{:S(2)}) copy-start(f32[4,2,256,256]{3,2,0,1:T(8,128)} %fusion.20) | copy-start | bytes 6291460
  64.6 7.1 %copy-start.3 = (f32[4,2,256,256]{3,2,0,1:T(8,128)S(1)}, f32[4,2,256,256]{3,2,0,1:T(8,128)}, u32[]{:S(2)}) copy-start(f32[4,2,256,256]{3,2,0,1:T(8,128)} %fusion.26) | copy-start | bytes 6291460
  64.6 7.7 %copy-start.4 = (f32[4,2,256,256]{3,2,1,0:T(8,128)S(1)}, f32[4,2,256,256]{3,2,1,0:T(8,128)}, u32[]{:S(2)}) copy-start(f32[4,2,256,256]{3,2,1,0:T(8,128)} %fusion.1) | copy-start | bytes 6291460
  64.6 7.7 %copy-start.7 = (f32[256,256]{1,0:T(8,128)S(1)}, f32[256,256]{1,0:T(8,128)}, u32[]{:S(2)}) copy-start(f32[256,256]{1,0:T(8,128)} %get-tuple-element.26) | copy-start | bytes 786436
  64.7 7.7 %copy-start.8 = (f32[256,256]{1,0:T(8,128)S(1)}, f32[256,256]{1,0:T(8,128)}, u32[]{:S(2)}) copy-start(f32[256,256]{1,0:T(8,128)} %get-tuple-element.27) | copy-start | bytes 786436
  64.7 7.8 %copy-start.9 = (f32[256,256]{1,0:T(8,128)S(1)}, f32[256,256]{1,0:T(8,128)}, u32[]{:S(2)}) copy-start(f32[256,256]{1,0:T(8,128)} %get-tuple-element.28) | copy-start | bytes 786436
  64.7 7.8 %copy-start.10 = (f32[256,256]{1,0:T(8,128)S(1)}, f32[256,256]{1,0:T(8,128)}, u32[]{:S(2)}) copy-start(f32[256,256]{1,0:T(8,128)} %get-tuple-element.29) | copy-start | bytes 786436
  64.7 7.9 %copy-start.11 = (f32[256,256]{1,0:T(8,128)S(1)}, f32[256,256]{1,0:T(8,128)}, u32[]{:S(2)}) copy-start(f32[256,256]{1,0:T(8,128)} %get-tuple-element.8) | copy-start | bytes 786436
  64.7 8.0 %copy-start.12 = (f32[256,256]{1,0:T(8,128)S(1)}, f32[256,256]{1,0:T(8,128)}, u32[]{:S(2)}) copy-start(f32[256,256]{1,0:T(8,128)} %get-tuple-element.9) | copy-start | bytes 786436
  64.7 8.0 %copy-start.13 = (f32[256,256]{1,0:T(8,128)S(1)}, f32[256,256]{1,0:T(8,128)}, u32[]{:S(2)}) copy-start(f32[256,256]{1,0:T(8,128)} %get-tuple-element.10) | copy-start | bytes 786436
  64.7 8.1 %copy-start.14 = (f32[256,256]{1,0:T(8,128)S(1)}, f32[256,256]{1,0:T(8,128)}, u32[]{:S(2)}) copy-start(f32[256,256]{1,0:T(8,128)} %get-tuple-element.11) | copy-start | bytes 786436
where the time goes:
time: 75.9 us; the launch traced here: 75.5 us
  waiting for transfers between devices  24.4 us (32%)
  matrix products  13.2 us (17%)
  other arithmetic  10.6 us (14%)
  starting transfers between devices  10.5 us (14%)
  local copies, waits for them, and re-layouts  8.72 us (11%)
  between operations  8.04 us (11%)
    ppermute x2, waiting for transfers between devices, passed_along_2(): lax.ppermute(x, axis, [(i, (i + by) % length) for i in range(length)])  24.4 us
    dot_general x6, matrix products, contribution(): jnp.dot(left_product.reshape(E_OUT * 2 * NO, NO), coupling[mode_index], p...  10.8 us
    another operation x3, other arithmetic, body(): jnp.stack([real_sum, imag_sum], axis=1).astype(jnp.bfloat16)[None, None]  7.07 us
    ppermute x2, starting transfers between devices, passed_along_2(): lax.ppermute(x, axis, [(i, (i + by) % length) for i in range(length)])  6.62 us
    ppermute x1, starting transfers between devices, passed_along(): return lax.ppermute(x, axis, pairs)  3.88 us
    unnamed x32, local copies, waits for them, and re-layouts  3.68 us
    dot_general x5, matrix products, contribution(): jnp.einsum('xy,ecyz->ecxz', coupling[mode_index], window, preferred_eleme...  2.35 us
    convert_element_type x2, other arithmetic, contribution(): product[:, 1] * weights[mode_index, 1]  2.13 us
  transfers between devices with their start and end apart: 3, of which 2 were waited for; matrix products, arithmetic and copies ran while one was open for 17% of the time, Pallas kernels for 0%

commit v1 on v0

v1 whole, which is shorter than its diff:
```python
import jax
import jax.numpy as jnp
from jax import lax
from jax.experimental import pallas as pl
from jax.experimental.pallas import tpu as pltpu
from jax.sharding import PartitionSpec as P

NO = 256
MODES = 2
E_OUT = 4
NOFF = 3
HALF = 128
STEP = 16
VMEM_LIMIT = 24 * 1024 * 1024
MESH = pl.DeviceIdType.MESH

CHUNKS = [(1, 0), (1, 1), (2, 0), (2, 1), (3, 0), (3, 1), (0, 0), (0, 1)]


def kernel(
    green, coupling, phonon, shift_in, out,
    shift, slots, couple, weights, prod, to_left, to_right, from_right, from_left, own,
    in_sem, below_sem, left_send, left_recv, right_send, right_recv,
):
    me = lax.axis_index("mom")
    points = lax.axis_size("mom")
    group = lax.axis_index("energy")
    groups = lax.axis_size("energy")
    left = lax.rem(me + points - 1, points)
    right = lax.rem(me + 1, points)
    has_below = group > 0
    has_above = group < groups - 1

    barrier = pltpu.get_barrier_semaphore()
    pl.semaphore_signal(barrier, inc=1, device_id={"mom": left}, device_id_type=MESH)
    pl.semaphore_signal(barrier, inc=1, device_id={"mom": right}, device_id_type=MESH)

    @pl.when(has_above)
    def _():
        pl.semaphore_signal(barrier, inc=1, device_id={"energy": group + 1}, device_id_type=MESH)

    @pl.when(has_below)
    def _():
        pl.semaphore_signal(barrier, inc=1, device_id={"energy": group - 1}, device_id_type=MESH)

    loads = {"shift": pltpu.make_async_copy(shift_in, shift, in_sem.at[E_OUT + 1 + NOFF])}
    loads["couple"] = pltpu.make_async_copy(coupling, couple, in_sem.at[0])
    for s in range(E_OUT):
        loads[s + 1] = pltpu.make_async_copy(green.at[s], slots.at[s + 1], in_sem.at[s + 1])
    for j in range(NOFF):
        loads["w", j] = pltpu.make_async_copy(phonon.at[j], weights.at[j], in_sem.at[E_OUT + 1 + j])
    order = ["shift", "couple", 1, 2, ("w", 0), ("w", 2), ("w", 1), 3, 4]
    for name in order:
        loads[name].start()
    waited = set()

    def need(name):
        if name not in waited:
            waited.add(name)
            loads[name].wait()

    below = pltpu.make_async_remote_copy(
        src_ref=green.at[E_OUT - 1],
        dst_ref=slots.at[0],
        send_sem=below_sem.at[0],
        recv_sem=below_sem.at[1],
        device_id={"energy": lax.rem(group + 1, groups)},
        device_id_type=MESH,
    )

    def products(s, half):
        rows = pl.ds(half * HALF, HALF)
        stacked = couple[:, rows, :].reshape(MODES * HALF, NO)
        for c in range(2):
            lefts = jnp.dot(stacked, slots[s, c], preferred_element_type=jnp.float32)
            lefts = lefts.astype(jnp.bfloat16)
            for a in range(MODES):
                prod[s, a, c, rows, :] = jnp.dot(
                    lefts[a * HALF:(a + 1) * HALF], couple[a], preferred_element_type=jnp.float32
                )

    def term(j, i, r):
        re = im = None
        for a in range(MODES):
            s = i + 1 - shift[a, j]
            p0 = prod[s, a, 0, pl.ds(r, STEP), :]
            p1 = prod[s, a, 1, pl.ds(r, STEP), :]
            d0 = weights[j, pl.ds(2 * a * NO + r, STEP), :].astype(jnp.float32)
            d1 = weights[j, pl.ds((2 * a + 1) * NO + r, STEP), :].astype(jnp.float32)
            one, two = p0 * d0 - p1 * d1, p0 * d1 + p1 * d0
            re = one if re is None else re + one
            im = two if im is None else im + two
        return re, im

    def over_rows(half, fn):
        def step(n, carry):
            fn(pl.multiple_of(half * HALF + n * STEP, STEP))
            return carry
        lax.fori_loop(0, HALF // STEP, step, 0)

    def sends(n, i, half):
        rows = pl.ds(half * HALF, HALF)
        a = pltpu.make_async_remote_copy(
            src_ref=to_left.at[i, :, rows, :], dst_ref=from_right.at[i, :, rows, :],
            send_sem=left_send.at[n], recv_sem=left_recv.at[n],
            device_id={"mom": left}, device_id_type=MESH)
        b = pltpu.make_async_remote_copy(
            src_ref=to_right.at[i, :, rows, :], dst_ref=from_left.at[i, :, rows, :],
            send_sem=right_send.at[n], recv_sem=right_recv.at[n],
            device_id={"mom": right}, device_id_type=MESH)
        return a, b

    have = set()
    copies = []
    for n, (i, half) in enumerate(CHUNKS):
        for s in (i + 1, i):
            if (s, half) in have:
                continue
            have.add((s, half))
            need("couple")
            if s > 0:
                need(s)
            elif half == 0:
                @pl.when(has_below)
                def _():
                    below.wait_recv()
            products(s, half)

        need("shift")
        need(("w", 0))
        need(("w", 2))

        def outer(r, i=i):
            re, im = term(0, i, r)
            to_left[i, 0, pl.ds(r, STEP), :] = re.astype(jnp.bfloat16)
            to_left[i, 1, pl.ds(r, STEP), :] = im.astype(jnp.bfloat16)
            re, im = term(2, i, r)
            to_right[i, 0, pl.ds(r, STEP), :] = re.astype(jnp.bfloat16)
            to_right[i, 1, pl.ds(r, STEP), :] = im.astype(jnp.bfloat16)

        over_rows(half, outer)

        need(("w", 1))

        def inner(r, i=i):
            re, im = term(1, i, r)
            own[i, 0, pl.ds(r, STEP), :] = re
            own[i, 1, pl.ds(r, STEP), :] = im

        if n > 0:
            over_rows(half, inner)
        else:
            pl.semaphore_wait(barrier, 2 + has_below.astype(jnp.int32) + has_above.astype(jnp.int32))

            @pl.when(has_above)
            def _():
                below.start()

            @pl.when(jnp.logical_not(has_below))
            def _():
                slots[0] = jnp.zeros((2, NO, NO), jnp.bfloat16)

        pair = sends(n, i, half)
        for copy in pair:
            copy.start()
        copies.append(pair)
        if n == 0:
            over_rows(half, inner)

    for n, (i, half) in enumerate(CHUNKS):
        for copy in copies[n]:
            copy.wait_recv()

        def final(r, i=i):
            for c in range(2):
                rows = pl.ds(r, STEP)
                total = own[i, c, rows, :] + from_right[i, c, rows, :].astype(jnp.float32)
                total = total + from_left[i, c, rows, :].astype(jnp.float32)
                out[i, c, rows, :] = total.astype(jnp.bfloat16)

        over_rows(half, final)

    for pair in copies:
        for copy in pair:
            copy.wait_send()

    @pl.when(has_above)
    def _():
        below.wait_send()


def body(green, coupling, phonon, shift):
    block = (E_OUT, 2, NO, NO)
    n = len(CHUNKS)
    result = pl.pallas_call(
        kernel,
        out_shape=jax.ShapeDtypeStruct(block, jnp.bfloat16),
        in_specs=[pl.BlockSpec(memory_space=pltpu.HBM)] * 4,
        out_specs=pl.BlockSpec(memory_space=pltpu.VMEM),
        scratch_shapes=[
            pltpu.SMEM((MODES, NOFF), jnp.int32),
            pltpu.VMEM((E_OUT + 1, 2, NO, NO), jnp.bfloat16),
            pltpu.VMEM((MODES, NO, NO), jnp.bfloat16),
            pltpu.VMEM((NOFF, MODES * 2 * NO, NO), jnp.bfloat16),
            pltpu.VMEM((E_OUT + 1, MODES, 2, NO, NO), jnp.float32),
            pltpu.VMEM(block, jnp.bfloat16),
            pltpu.VMEM(block, jnp.bfloat16),
            pltpu.VMEM(block, jnp.bfloat16),
            pltpu.VMEM(block, jnp.bfloat16),
            pltpu.VMEM(block, jnp.float32),
            pltpu.SemaphoreType.DMA((E_OUT + 2 + NOFF,)),
            pltpu.SemaphoreType.DMA((2,)),
            pltpu.SemaphoreType.DMA((n,)),
            pltpu.SemaphoreType.DMA((n,)),
            pltpu.SemaphoreType.DMA((n,)),
            pltpu.SemaphoreType.DMA((n,)),
        ],
        compiler_params=pltpu.CompilerParams(
            collective_id=0, has_side_effects=True, vmem_limit_bytes=VMEM_LIMIT
        ),
    )(
        pltpu.with_memory_space_constraint(green.reshape(block), pltpu.HBM),
        pltpu.with_memory_space_constraint(coupling, pltpu.HBM),
        pltpu.with_memory_space_constraint(phonon, pltpu.HBM),
        pltpu.with_memory_space_constraint(shift.T, pltpu.HBM),
    )
    return result.reshape((1, 1) + block)


def solution(mesh):
    placed = (P("mom", "energy", None, None, None, None), P(), P(), P())
    return jax.shard_map(
        body,
        mesh=mesh,
        in_specs=placed,
        out_specs=P("mom", "energy", None, None, None, None),
        check_vma=False,
    )
```

time: 75.9 us -> 39.4 us (0.52)
  the two profiles are of different devices: /device:TPU:287 before, /device:TPU:2 now
where the time goes in v1:
time: 39.4 us; the launch traced here: 39.2 us
  Pallas kernels  38.2 us (97%)
  local copies, waits for them, and re-layouts  0.97 us (2%)
    pallas_call x1, Pallas kernels, body(): pl.pallas_call(kernel, out_shape=jax.ShapeDtypeStruct(block, jnp.bfloat16...  38.2 us
    unnamed x1, local copies, waits for them, and re-layouts  0.97 us

profile of v1, /device:TPU:2, one launch (start us, length us, event | category | flops | bytes accessed | tf_op | source)
XLA Modules:
  0.0 39.2 jit_solution(11006308630685231126)
XLA Ops:
  0.0 38.2 %shard_map.46 = bf16[4,2,256,256]{3,2,1,0:T(8,128)(2,1)S(1)} custom-call(bf16[4,2,256,256]{3,2,1,0:T(8,128)(2,1)} %bitcast.4, bf16[2,256,256]{2,1,0:T(8,128)(2,1)} %coupling.1, bf16[3,1024,256]{2,1,0:T(8,128)(2,1)} %phonon.1, s32[2,3]{1,0:T(2,128)} %bitcast.5), custom_call_target="tpu_custom_call" | custom-call | tf_op jit(solution)/shard_map/pallas_call | solution.py:195
  38.2 1.0 %copy.6 = bf16[1,1,4,2,256,256]{5,4,3,2,1,0:T(8,128)(2,1)} copy(bf16[1,1,4,2,256,256]{5,4,3,2,1,0:T(8,128)(2,1)S(1)} %bitcast.3) | data formatting | bytes 2097152

commit v2 on v1

--- a/solution.py
+++ b/solution.py
@@ -11,6 +11,8 @@
 NOFF = 3
 HALF = 128
 STEP = 16
+EDGE = 16
+DETOUR = 3
 VMEM_LIMIT = 24 * 1024 * 1024
 MESH = pl.DeviceIdType.MESH
 
@@ -20,7 +22,7 @@
 def kernel(
     green, coupling, phonon, shift_in, out,
     shift, slots, couple, weights, prod, to_left, to_right, from_right, from_left, own,
-    in_sem, below_sem, left_send, left_recv, right_send, right_recv,
+    relay, in_sem, below_sem, relay_sem, left_send, left_recv, right_send, right_recv,
 ):
     me = lax.axis_index("mom")
     points = lax.axis_size("mom")
@@ -31,17 +33,30 @@
     has_below = group > 0
     has_above = group < groups - 1
 
+    detoured = (me == points // 2 - 1) | (me == points // 2)
+    place = lax.rem(group, EDGE)
+    detour_up = detoured & has_above & (place == EDGE - 1)
+    detour_over = detoured & (group >= EDGE) & (place == DETOUR - 1)
+    detour_down = detoured & has_below & (place == 0)
+    direct_up = has_above & jnp.logical_not(detour_up)
+    direct_down = has_below & jnp.logical_not(detour_down)
+    over = lax.rem(group + DETOUR, groups)
+
     barrier = pltpu.get_barrier_semaphore()
     pl.semaphore_signal(barrier, inc=1, device_id={"mom": left}, device_id_type=MESH)
     pl.semaphore_signal(barrier, inc=1, device_id={"mom": right}, device_id_type=MESH)
 
-    @pl.when(has_above)
-    def _():
-        pl.semaphore_signal(barrier, inc=1, device_id={"energy": group + 1}, device_id_type=MESH)
-
-    @pl.when(has_below)
+    @pl.when(direct_down)
     def _():
         pl.semaphore_signal(barrier, inc=1, device_id={"energy": group - 1}, device_id_type=MESH)
+
+    @pl.when(detour_over)
+    def _():
+        pl.semaphore_signal(barrier, inc=1, device_id={"energy": group - DETOUR}, device_id_type=MESH)
+
+    @pl.when(detour_down)
+    def _():
+        pl.semaphore_signal(barrier, inc=1, device_id={"energy": group + DETOUR - 1}, device_id_type=MESH)
 
     loads = {"shift": pltpu.make_async_copy(shift_in, shift, in_sem.at[E_OUT + 1 + NOFF])}
     loads["couple"] = pltpu.make_async_copy(coupling, couple, in_sem.at[0])
@@ -65,6 +80,23 @@
         send_sem=below_sem.at[0],
         recv_sem=below_sem.at[1],
         device_id={"energy": lax.rem(group + 1, groups)},
+        device_id_type=MESH,
+    )
+
+    out_of_way = pltpu.make_async_remote_copy(
+        src_ref=green.at[E_OUT - 1],
+        dst_ref=relay,
+        send_sem=relay_sem.at[0],
+        recv_sem=relay_sem.at[1],
+        device_id={"energy": over},
+        device_id_type=MESH,
+    )
+    back = pltpu.make_async_remote_copy(
+        src_ref=relay,
+        dst_ref=slots.at[0],
+        send_sem=relay_sem.at[2],
+        recv_sem=below_sem.at[1],
+        device_id={"energy": lax.rem(group + groups - DETOUR + 1, groups)},
         device_id_type=MESH,
     )
 
@@ -121,6 +153,11 @@
             if s > 0:
                 need(s)
             elif half == 0:
+                @pl.when(detour_over)
+                def _():
+                    out_of_way.wait_recv()
+                    back.start()
+
                 @pl.when(has_below)
                 def _():
                     below.wait_recv()
@@ -150,11 +187,15 @@
         if n > 0:
             over_rows(half, inner)
         else:
-            pl.semaphore_wait(barrier, 2 + has_below.astype(jnp.int32) + has_above.astype(jnp.int32))
-
-            @pl.when(has_above)
+            pl.semaphore_wait(barrier, 2 + has_above.astype(jnp.int32) + detour_over.astype(jnp.int32))
+
+            @pl.when(direct_up)
             def _():
                 below.start()
+
+            @pl.when(detour_up)
+            def _():
+                out_of_way.start()
 
             @pl.when(jnp.logical_not(has_below))
             def _():
@@ -184,9 +225,17 @@
         for copy in pair:
             copy.wait_send()
 
-    @pl.when(has_above)
+    @pl.when(direct_up)
     def _():
         below.wait_send()
+
+    @pl.when(detour_up)
+    def _():
+        out_of_way.wait_send()
+
+    @pl.when(detour_over)
+    def _():
+        back.wait_send()
 
 
 def body(green, coupling, phonon, shift):
@@ -208,8 +257,10 @@
             pltpu.VMEM(block, jnp.bfloat16),
             pltpu.VMEM(block, jnp.bfloat16),
             pltpu.VMEM(block, jnp.float32),
+            pltpu.VMEM((2, NO, NO), jnp.bfloat16),
             pltpu.SemaphoreType.DMA((E_OUT + 2 + NOFF,)),
             pltpu.SemaphoreType.DMA((2,)),
+            pltpu.SemaphoreType.DMA((3,)),
             pltpu.SemaphoreType.DMA((n,)),
             pltpu.SemaphoreType.DMA((n,)),
             pltpu.SemaphoreType.DMA((n,)),

time: 39.4 us -> 34.4 us (0.87)
  the two profiles are of different devices: /device:TPU:2 before, /device:TPU:49 now
where the time goes in v2:
time: 34.4 us; the launch traced here: 34.2 us
  Pallas kernels  33.2 us (97%)
  local copies, waits for them, and re-layouts  0.97 us (3%)
    pallas_call x1, Pallas kernels, body(): pl.pallas_call(kernel, out_shape=jax.ShapeDtypeStruct(block, jnp.bfloat16...  33.2 us
    unnamed x1, local copies, waits for them, and re-layouts  0.97 us

profile of v2, /device:TPU:49, one launch (start us, length us, event | category | flops | bytes accessed | tf_op | source)
XLA Modules:
  0.0 34.2 jit_solution(14190245706593654864)
XLA Ops:
  0.0 33.2 %shard_map.46 = bf16[4,2,256,256]{3,2,1,0:T(8,128)(2,1)S(1)} custom-call(bf16[4,2,256,256]{3,2,1,0:T(8,128)(2,1)} %bitcast.4, bf16[2,256,256]{2,1,0:T(8,128)(2,1)} %coupling.1, bf16[3,1024,256]{2,1,0:T(8,128)(2,1)} %phonon.1, s32[2,3]{1,0:T(2,128)} %bitcast.5), custom_call_target="tpu_custom_call" | custom-call | tf_op jit(solution)/shard_map/pallas_call | solution.py:244
  33.2 1.0 %copy.6 = bf16[1,1,4,2,256,256]{5,4,3,2,1,0:T(8,128)(2,1)} copy(bf16[1,1,4,2,256,256]{5,4,3,2,1,0:T(8,128)(2,1)S(1)} %bitcast.3) | data formatting | bytes 2097152

commit v3 on v2

--- a/solution.py
+++ b/solution.py
@@ -22,7 +22,7 @@
 def kernel(
     green, coupling, phonon, shift_in, out,
     shift, slots, couple, weights, prod, to_left, to_right, from_right, from_left, own,
-    relay, in_sem, below_sem, relay_sem, left_send, left_recv, right_send, right_recv,
+    relay, in_sem, below_sem, relay_sem, ready, left_send, left_recv, right_send, right_recv,
 ):
     me = lax.axis_index("mom")
     points = lax.axis_size("mom")
@@ -42,11 +42,24 @@
     direct_down = has_below & jnp.logical_not(detour_down)
     over = lax.rem(group + DETOUR, groups)
 
+    last = me == points - 1
+    feeder = me == points - 2
+
+    def tell(semaphore, device):
+        pl.semaphore_signal(semaphore, inc=1, device_id=device, device_id_type=MESH)
+
     barrier = pltpu.get_barrier_semaphore()
     pl.semaphore_signal(barrier, inc=1, device_id={"mom": left}, device_id_type=MESH)
-    pl.semaphore_signal(barrier, inc=1, device_id={"mom": right}, device_id_type=MESH)
-
-    @pl.when(direct_down)
+
+    @pl.when(jnp.logical_not(feeder))
+    def _():
+        pl.semaphore_signal(barrier, inc=1, device_id={"mom": right}, device_id_type=MESH)
+
+    @pl.when(feeder & has_above)
+    def _():
+        pl.semaphore_signal(barrier, inc=1, device_id={"energy": group + 1}, device_id_type=MESH)
+
+    @pl.when(direct_down & jnp.logical_not(last))
     def _():
         pl.semaphore_signal(barrier, inc=1, device_id={"energy": group - 1}, device_id_type=MESH)
 
@@ -58,14 +71,18 @@
     def _():
         pl.semaphore_signal(barrier, inc=1, device_id={"energy": group + DETOUR - 1}, device_id_type=MESH)
 
-    loads = {"shift": pltpu.make_async_copy(shift_in, shift, in_sem.at[E_OUT + 1 + NOFF])}
+    loads = {"shift": pltpu.make_async_copy(shift_in, shift, in_sem.at[E_OUT + 1])}
     loads["couple"] = pltpu.make_async_copy(coupling, couple, in_sem.at[0])
     for s in range(E_OUT):
         loads[s + 1] = pltpu.make_async_copy(green.at[s], slots.at[s + 1], in_sem.at[s + 1])
     for j in range(NOFF):
-        loads["w", j] = pltpu.make_async_copy(phonon.at[j], weights.at[j], in_sem.at[E_OUT + 1 + j])
-    order = ["shift", "couple", 1, 2, ("w", 0), ("w", 2), ("w", 1), 3, 4]
-    for name in order:
+        for half in range(2):
+            rows = pl.ds(half * HALF, HALF)
+            loads["w", j, half] = pltpu.make_async_copy(
+                phonon.at[j, :, rows, :], weights.at[j, :, rows, :], in_sem.at[E_OUT + 2 + 2 * j + half])
+    first = ["shift", "couple", 2, 1, ("w", 2, 0), ("w", 0, 0)]
+    rest = [("w", 1, 0), 3, ("w", 2, 1), ("w", 0, 1), ("w", 1, 1), 4]
+    for name in first:
         loads[name].start()
     waited = set()
 
@@ -117,8 +134,8 @@
             s = i + 1 - shift[a, j]
             p0 = prod[s, a, 0, pl.ds(r, STEP), :]
             p1 = prod[s, a, 1, pl.ds(r, STEP), :]
-            d0 = weights[j, pl.ds(2 * a * NO + r, STEP), :].astype(jnp.float32)
-            d1 = weights[j, pl.ds((2 * a + 1) * NO + r, STEP), :].astype(jnp.float32)
+            d0 = weights[j, 2 * a, pl.ds(r, STEP), :].astype(jnp.float32)
+            d1 = weights[j, 2 * a + 1, pl.ds(r, STEP), :].astype(jnp.float32)
             one, two = p0 * d0 - p1 * d1, p0 * d1 + p1 * d0
             re = one if re is None else re + one
             im = two if im is None else im + two
@@ -153,6 +170,16 @@
             if s > 0:
                 need(s)
             elif half == 0:
+                @pl.when(feeder & has_above)
+                def _():
+                    pl.semaphore_wait(ready.at[1], 1)
+                    tell(ready.at[2], {"mom": right})
+
+                @pl.when(last & has_above)
+                def _():
+                    pl.semaphore_wait(ready.at[2], 1)
+                    below.start()
+
                 @pl.when(detour_over)
                 def _():
                     out_of_way.wait_recv()
@@ -164,8 +191,11 @@
             products(s, half)
 
         need("shift")
-        need(("w", 0))
-        need(("w", 2))
+        need(("w", 2, half))
+        need(("w", 0, half))
+        if n == 0:
+            for name in rest:
+                loads[name].start()
 
         def outer(r, i=i):
             re, im = term(0, i, r)
@@ -177,19 +207,42 @@
 
         over_rows(half, outer)
 
-        need(("w", 1))
-
         def inner(r, i=i):
             re, im = term(1, i, r)
             own[i, 0, pl.ds(r, STEP), :] = re
             own[i, 1, pl.ds(r, STEP), :] = im
 
+        to_the_left, to_the_right = sends(n, i, half)
+        copies.append((to_the_left, to_the_right))
         if n > 0:
+            need(("w", 1, half))
             over_rows(half, inner)
+            to_the_right.start()
+            if n == 1:
+                @pl.when(last)
+                def _():
+                    pl.semaphore_wait(ready.at[0], 1)
+                    copies[0][0].start()
+            to_the_left.start()
         else:
-            pl.semaphore_wait(barrier, 2 + has_above.astype(jnp.int32) + detour_over.astype(jnp.int32))
-
-            @pl.when(direct_up)
+            waits = 2 + has_above.astype(jnp.int32) + detour_over.astype(jnp.int32)
+            waits = waits + (feeder & has_below).astype(jnp.int32)
+            pl.semaphore_wait(barrier, jnp.where(last, 1, waits))
+            to_the_right.start()
+
+            @pl.when(jnp.logical_not(last))
+            def _():
+                to_the_left.start()
+
+            @pl.when(feeder)
+            def _():
+                tell(ready.at[0], {"mom": right})
+
+            @pl.when(feeder & has_below)
+            def _():
+                tell(ready.at[1], {"energy": group - 1})
+
+            @pl.when(direct_up & jnp.logical_not(last))
             def _():
                 below.start()
 
@@ -201,11 +254,7 @@
             def _():
                 slots[0] = jnp.zeros((2, NO, NO), jnp.bfloat16)
 
-        pair = sends(n, i, half)
-        for copy in pair:
-            copy.start()
-        copies.append(pair)
-        if n == 0:
+            need(("w", 1, half))
             over_rows(half, inner)
 
     for n, (i, half) in enumerate(CHUNKS):
@@ -250,7 +299,7 @@
             pltpu.SMEM((MODES, NOFF), jnp.int32),
             pltpu.VMEM((E_OUT + 1, 2, NO, NO), jnp.bfloat16),
             pltpu.VMEM((MODES, NO, NO), jnp.bfloat16),
-            pltpu.VMEM((NOFF, MODES * 2 * NO, NO), jnp.bfloat16),
+            pltpu.VMEM((NOFF, MODES * 2, NO, NO), jnp.bfloat16),
             pltpu.VMEM((E_OUT + 1, MODES, 2, NO, NO), jnp.float32),
             pltpu.VMEM(block, jnp.bfloat16),
             pltpu.VMEM(block, jnp.bfloat16),
@@ -258,9 +307,10 @@
             pltpu.VMEM(block, jnp.bfloat16),
             pltpu.VMEM(block, jnp.float32),
             pltpu.VMEM((2, NO, NO), jnp.bfloat16),
-            pltpu.SemaphoreType.DMA((E_OUT + 2 + NOFF,)),
+            pltpu.SemaphoreType.DMA((E_OUT + 2 + 2 * NOFF,)),
             pltpu.SemaphoreType.DMA((2,)),
             pltpu.SemaphoreType.DMA((3,)),
+            pltpu.SemaphoreType.REGULAR((3,)),
             pltpu.SemaphoreType.DMA((n,)),
             pltpu.SemaphoreType.DMA((n,)),
             pltpu.SemaphoreType.DMA((n,)),
@@ -272,7 +322,7 @@
     )(
         pltpu.with_memory_space_constraint(green.reshape(block), pltpu.HBM),
         pltpu.with_memory_space_constraint(coupling, pltpu.HBM),
-        pltpu.with_memory_space_constraint(phonon, pltpu.HBM),
+        pltpu.with_memory_space_constraint(phonon.reshape(NOFF, MODES * 2, NO, NO), pltpu.HBM),
         pltpu.with_memory_space_constraint(shift.T, pltpu.HBM),
     )
     return result.reshape((1, 1) + block)

time: 34.4 us -> 33.6 us (0.977)
  the two profiles are of different devices: /device:TPU:49 before, /device:TPU:2 now
where the time goes in v3:
time: 33.6 us; the launch traced here: 33.5 us
  Pallas kernels  32.5 us (97%)
  local copies, waits for them, and re-layouts  0.97 us (3%)
    pallas_call x1, Pallas kernels, body(): pl.pallas_call(kernel, out_shape=jax.ShapeDtypeStruct(block, jnp.bfloat16...  32.5 us
    unnamed x1, local copies, waits for them, and re-layouts  0.97 us

profile of v3, /device:TPU:2, one launch (start us, length us, event | category | flops | bytes accessed | tf_op | source)
XLA Modules:
  0.0 33.5 jit_solution(5253424916882761771)
XLA Ops:
  0.0 32.5 %shard_map.46 = bf16[4,2,256,256]{3,2,1,0:T(8,128)(2,1)S(1)} custom-call(bf16[4,2,256,256]{3,2,1,0:T(8,128)(2,1)} %bitcast.6, bf16[2,256,256]{2,1,0:T(8,128)(2,1)} %coupling.1, bf16[3,4,256,256]{3,2,1,0:T(8,128)(2,1)} %bitcast.5, s32[2,3]{1,0:T(2,128)} %bitcast.7), custom_call_target="tpu_custom_call" | custom-call | tf_op jit(solution)/shard_map/pallas_call | solution.py:293
  32.5 1.0 %copy.6 = bf16[1,1,4,2,256,256]{5,4,3,2,1,0:T(8,128)(2,1)} copy(bf16[1,1,4,2,256,256]{5,4,3,2,1,0:T(8,128)(2,1)S(1)} %bitcast.4) | data formatting | bytes 2097152

commit v4 on v3

--- a/solution.py
+++ b/solution.py
@@ -1,3 +1,5 @@
+import functools
+
 import jax
 import jax.numpy as jnp
 from jax import lax
@@ -13,6 +15,7 @@
 STEP = 16
 EDGE = 16
 DETOUR = 3
+GAP = 32
 VMEM_LIMIT = 24 * 1024 * 1024
 MESH = pl.DeviceIdType.MESH
 
@@ -24,53 +27,6 @@
     shift, slots, couple, weights, prod, to_left, to_right, from_right, from_left, own,
     relay, in_sem, below_sem, relay_sem, ready, left_send, left_recv, right_send, right_recv,
 ):
-    me = lax.axis_index("mom")
-    points = lax.axis_size("mom")
-    group = lax.axis_index("energy")
-    groups = lax.axis_size("energy")
-    left = lax.rem(me + points - 1, points)
-    right = lax.rem(me + 1, points)
-    has_below = group > 0
-    has_above = group < groups - 1
-
-    detoured = (me == points // 2 - 1) | (me == points // 2)
-    place = lax.rem(group, EDGE)
-    detour_up = detoured & has_above & (place == EDGE - 1)
-    detour_over = detoured & (group >= EDGE) & (place == DETOUR - 1)
-    detour_down = detoured & has_below & (place == 0)
-    direct_up = has_above & jnp.logical_not(detour_up)
-    direct_down = has_below & jnp.logical_not(detour_down)
-    over = lax.rem(group + DETOUR, groups)
-
-    last = me == points - 1
-    feeder = me == points - 2
-
-    def tell(semaphore, device):
-        pl.semaphore_signal(semaphore, inc=1, device_id=device, device_id_type=MESH)
-
-    barrier = pltpu.get_barrier_semaphore()
-    pl.semaphore_signal(barrier, inc=1, device_id={"mom": left}, device_id_type=MESH)
-
-    @pl.when(jnp.logical_not(feeder))
-    def _():
-        pl.semaphore_signal(barrier, inc=1, device_id={"mom": right}, device_id_type=MESH)
-
-    @pl.when(feeder & has_above)
-    def _():
-        pl.semaphore_signal(barrier, inc=1, device_id={"energy": group + 1}, device_id_type=MESH)
-
-    @pl.when(direct_down & jnp.logical_not(last))
-    def _():
-        pl.semaphore_signal(barrier, inc=1, device_id={"energy": group - 1}, device_id_type=MESH)
-
-    @pl.when(detour_over)
-    def _():
-        pl.semaphore_signal(barrier, inc=1, device_id={"energy": group - DETOUR}, device_id_type=MESH)
-
-    @pl.when(detour_down)
-    def _():
-        pl.semaphore_signal(barrier, inc=1, device_id={"energy": group + DETOUR - 1}, device_id_type=MESH)
-
     loads = {"shift": pltpu.make_async_copy(shift_in, shift, in_sem.at[E_OUT + 1])}
     loads["couple"] = pltpu.make_async_copy(coupling, couple, in_sem.at[0])
     for s in range(E_OUT):
@@ -84,6 +40,53 @@
     rest = [("w", 1, 0), 3, ("w", 2, 1), ("w", 0, 1), ("w", 1, 1), 4]
     for name in first:
         loads[name].start()
+    me = lax.axis_index("mom")
+    points = lax.axis_size("mom")
+    group = lax.axis_index("energy")
+    groups = lax.axis_size("energy")
+    left = lax.rem(me + points - 1, points)
+    right = lax.rem(me + 1, points)
+    has_below = group > 0
+    has_above = group < groups - 1
+
+    detoured = (me == points // 2 - 1) | (me == points // 2)
+    place = lax.rem(group, EDGE)
+    detour_up = detoured & has_above & (place == EDGE - 1)
+    detour_over = detoured & (group >= EDGE) & (place == DETOUR - 1)
+    detour_down = detoured & has_below & (place == 0)
+    direct_up = has_above & jnp.logical_not(detour_up)
+    direct_down = has_below & jnp.logical_not(detour_down)
+    over = lax.rem(group + DETOUR, groups)
+
+    last = me == points - 1
+    feeder = me == points - 2
+
+    def tell(semaphore, device):
+        pl.semaphore_signal(semaphore, inc=1, device_id=device, device_id_type=MESH)
+
+    barrier = pltpu.get_barrier_semaphore()
+    pl.semaphore_signal(barrier, inc=1, device_id={"mom": left}, device_id_type=MESH)
+
+    @pl.when(jnp.logical_not(feeder))
+    def _():
+        pl.semaphore_signal(barrier, inc=1, device_id={"mom": right}, device_id_type=MESH)
+
+    @pl.when(feeder & has_above)
+    def _():
+        pl.semaphore_signal(barrier, inc=1, device_id={"energy": group + 1}, device_id_type=MESH)
+
+    @pl.when(direct_down & jnp.logical_not(last))
+    def _():
+        pl.semaphore_signal(barrier, inc=1, device_id={"energy": group - 1}, device_id_type=MESH)
+
+    @pl.when(detour_over)
+    def _():
+        pl.semaphore_signal(barrier, inc=1, device_id={"energy": group - DETOUR}, device_id_type=MESH)
+
+    @pl.when(detour_down)
+    def _():
+        pl.semaphore_signal(barrier, inc=1, device_id={"energy": group + DETOUR - 1}, device_id_type=MESH)
+
     waited = set()
 
     def need(name):
@@ -141,11 +144,11 @@
             im = two if im is None else im + two
         return re, im
 
-    def over_rows(half, fn):
+    def over_rows(half, fn, begin=0, end=HALF):
         def step(n, carry):
             fn(pl.multiple_of(half * HALF + n * STEP, STEP))
             return carry
-        lax.fori_loop(0, HALF // STEP, step, 0)
+        lax.fori_loop(begin // STEP, end // STEP, step, 0)
 
     def sends(n, i, half):
         rows = pl.ds(half * HALF, HALF)
@@ -158,6 +161,11 @@
             send_sem=right_send.at[n], recv_sem=right_recv.at[n],
             device_id={"mom": right}, device_id_type=MESH)
         return a, b
+
+    def inner(r, i):
+        re, im = term(1, i, r)
+        own[i, 0, pl.ds(r, STEP), :] = re
+        own[i, 1, pl.ds(r, STEP), :] = im
 
     have = set()
     copies = []
@@ -207,16 +215,12 @@
 
         over_rows(half, outer)
 
-        def inner(r, i=i):
-            re, im = term(1, i, r)
-            own[i, 0, pl.ds(r, STEP), :] = re
-            own[i, 1, pl.ds(r, STEP), :] = im
-
         to_the_left, to_the_right = sends(n, i, half)
         copies.append((to_the_left, to_the_right))
         if n > 0:
-            need(("w", 1, half))
-            over_rows(half, inner)
+            for h in {0, half}:
+                need(("w", 1, h))
+            over_rows(half, functools.partial(inner, i=i), 0, GAP)
             to_the_right.start()
             if n == 1:
                 @pl.when(last)
@@ -254,8 +258,9 @@
             def _():
                 slots[0] = jnp.zeros((2, NO, NO), jnp.bfloat16)
 
-            need(("w", 1, half))
-            over_rows(half, inner)
+
+    for n, (i, half) in enumerate(CHUNKS):
+        over_rows(half, functools.partial(inner, i=i), GAP if n > 0 else 0)
 
     for n, (i, half) in enumerate(CHUNKS):
         for copy in copies[n]:

time: 33.6 us -> 33.3 us (level)
  the two profiles are of different devices: /device:TPU:2 before, /device:TPU:320 now
where the time goes in v4:
time: 33.3 us; the launch traced here: 33.1 us
  Pallas kernels  32.1 us (96%)
  local copies, waits for them, and re-layouts  0.97 us (3%)
    pallas_call x1, Pallas kernels, body(): pl.pallas_call(kernel, out_shape=jax.ShapeDtypeStruct(block, jnp.bfloat16...  32.1 us
    unnamed x1, local copies, waits for them, and re-layouts  0.97 us

profile of v4, /device:TPU:320, one launch (start us, length us, event | category | flops | bytes accessed | tf_op | source)
XLA Modules:
  0.0 33.1 jit_solution(2967106333073296625)
XLA Ops:
  0.0 32.1 %shard_map.46 = bf16[4,2,256,256]{3,2,1,0:T(8,128)(2,1)S(1)} custom-call(bf16[4,2,256,256]{3,2,1,0:T(8,128)(2,1)} %bitcast.6, bf16[2,256,256]{2,1,0:T(8,128)(2,1)} %coupling.1, bf16[3,4,256,256]{3,2,1,0:T(8,128)(2,1)} %bitcast.5, s32[2,3]{1,0:T(2,128)} %bitcast.7), custom_call_target="tpu_custom_call" | custom-call | tf_op jit(solution)/shard_map/pallas_call | solution.py:298
  32.1 1.0 %copy.6 = bf16[1,1,4,2,256,256]{5,4,3,2,1,0:T(8,128)(2,1)} copy(bf16[1,1,4,2,256,256]{5,4,3,2,1,0:T(8,128)(2,1)S(1)} %bitcast.4) | data formatting | bytes 2097152

commit v5 on v4

--- a/solution.py
+++ b/solution.py
@@ -167,6 +167,11 @@
         own[i, 0, pl.ds(r, STEP), :] = re
         own[i, 1, pl.ds(r, STEP), :] = im
 
+    def weigh(r, j, i, target):
+        re, im = term(j, i, r)
+        target[i, 0, pl.ds(r, STEP), :] = re.astype(jnp.bfloat16)
+        target[i, 1, pl.ds(r, STEP), :] = im.astype(jnp.bfloat16)
+
     have = set()
     copies = []
     for n, (i, half) in enumerate(CHUNKS):
@@ -205,23 +210,16 @@
             for name in rest:
                 loads[name].start()
 
-        def outer(r, i=i):
-            re, im = term(0, i, r)
-            to_left[i, 0, pl.ds(r, STEP), :] = re.astype(jnp.bfloat16)
-            to_left[i, 1, pl.ds(r, STEP), :] = im.astype(jnp.bfloat16)
-            re, im = term(2, i, r)
-            to_right[i, 0, pl.ds(r, STEP), :] = re.astype(jnp.bfloat16)
-            to_right[i, 1, pl.ds(r, STEP), :] = im.astype(jnp.bfloat16)
-
-        over_rows(half, outer)
-
+        over_rows(half, functools.partial(weigh, j=2, i=i, target=to_right))
+        go_left = functools.partial(weigh, j=0, i=i, target=to_left)
+        over_rows(half, go_left, 0, GAP)
         to_the_left, to_the_right = sends(n, i, half)
         copies.append((to_the_left, to_the_right))
         if n > 0:
-            for h in {0, half}:
-                need(("w", 1, h))
+            need(("w", 1, half))
+            to_the_right.start()
+            over_rows(half, go_left, GAP)
             over_rows(half, functools.partial(inner, i=i), 0, GAP)
-            to_the_right.start()
             if n == 1:
                 @pl.when(last)
                 def _():
@@ -233,6 +231,9 @@
             waits = waits + (feeder & has_below).astype(jnp.int32)
             pl.semaphore_wait(barrier, jnp.where(last, 1, waits))
             to_the_right.start()
+            over_rows(half, go_left, GAP)
+            need(("w", 1, half))
+            over_rows(half, functools.partial(inner, i=i), 0, GAP)
 
             @pl.when(jnp.logical_not(last))
             def _():
@@ -260,7 +261,7 @@
 
 
     for n, (i, half) in enumerate(CHUNKS):
-        over_rows(half, functools.partial(inner, i=i), GAP if n > 0 else 0)
+        over_rows(half, functools.partial(inner, i=i), GAP)
 
     for n, (i, half) in enumerate(CHUNKS):
         for copy in copies[n]:

time: 33.3 us -> 33.4 us (level)
  the two profiles are of different devices: /device:TPU:320 before, /device:TPU:2 now
where the time goes in v5:
time: 33.4 us; the launch traced here: 33.2 us
  Pallas kernels  32.2 us (96%)
  local copies, waits for them, and re-layouts  0.97 us (3%)
    pallas_call x1, Pallas kernels, body(): pl.pallas_call(kernel, out_shape=jax.ShapeDtypeStruct(block, jnp.bfloat16...  32.2 us
    unnamed x1, local copies, waits for them, and re-layouts  0.97 us

profile of v5, /device:TPU:2, one launch (start us, length us, event | category | flops | bytes accessed | tf_op | source)
XLA Modules:
  0.0 33.2 jit_solution(7920749958497448788)
XLA Ops:
  0.0 32.2 %shard_map.46 = bf16[4,2,256,256]{3,2,1,0:T(8,128)(2,1)S(1)} custom-call(bf16[4,2,256,256]{3,2,1,0:T(8,128)(2,1)} %bitcast.6, bf16[2,256,256]{2,1,0:T(8,128)(2,1)} %coupling.1, bf16[3,4,256,256]{3,2,1,0:T(8,128)(2,1)} %bitcast.5, s32[2,3]{1,0:T(2,128)} %bitcast.7), custom_call_target="tpu_custom_call" | custom-call | tf_op jit(solution)/shard_map/pallas_call | solution.py:299
  32.2 1.0 %copy.6 = bf16[1,1,4,2,256,256]{5,4,3,2,1,0:T(8,128)(2,1)} copy(bf16[1,1,4,2,256,256]{5,4,3,2,1,0:T(8,128)(2,1)S(1)} %bitcast.4) | data formatting | bytes 2097152

commit v6 on v5

--- a/solution.py
+++ b/solution.py
@@ -15,7 +15,7 @@
 STEP = 16
 EDGE = 16
 DETOUR = 3
-GAP = 32
+GAP = 16
 VMEM_LIMIT = 24 * 1024 * 1024
 MESH = pl.DeviceIdType.MESH
 

time: 33.4 us -> 33.3 us (level)
  no operation moved by 1% of the time
where the time goes in v6:
time: 33.3 us; the launch traced here: 33.2 us
  Pallas kernels  32.2 us (97%)
  local copies, waits for them, and re-layouts  0.97 us (3%)
    pallas_call x1, Pallas kernels, body(): pl.pallas_call(kernel, out_shape=jax.ShapeDtypeStruct(block, jnp.bfloat16...  32.2 us
    unnamed x1, local copies, waits for them, and re-layouts  0.97 us

profile of v6, /device:TPU:2, one launch (start us, length us, event | category | flops | bytes accessed | tf_op | source)
XLA Modules:
  0.0 33.2 jit_solution(11721381073673013918)
XLA Ops:
  0.0 32.2 %shard_map.46 = bf16[4,2,256,256]{3,2,1,0:T(8,128)(2,1)S(1)} custom-call(bf16[4,2,256,256]{3,2,1,0:T(8,128)(2,1)} %bitcast.6, bf16[2,256,256]{2,1,0:T(8,128)(2,1)} %coupling.1, bf16[3,4,256,256]{3,2,1,0:T(8,128)(2,1)} %bitcast.5, s32[2,3]{1,0:T(2,128)} %bitcast.7), custom_call_target="tpu_custom_call" | custom-call | tf_op jit(solution)/shard_map/pallas_call | solution.py:299
  32.2 1.0 %copy.6 = bf16[1,1,4,2,256,256]{5,4,3,2,1,0:T(8,128)(2,1)} copy(bf16[1,1,4,2,256,256]{5,4,3,2,1,0:T(8,128)(2,1)S(1)} %bitcast.4) | data formatting | bytes 2097152
